TPU v7x, 32 devices: a whole 2x2x4 slice. The times are simulated.
32 devices in a mesh: grp: 4 (over y, core), blk: 8 (over z, x).
Axes of the slice: x: 2, y: 2, z: 4, core: 2. Of those that a mesh axis runs over, the one named last changes fastest.
Arguments:
- child_field: bfloat16 [32768, 384], P(('grp', 'blk')), may hold values from -6 to 6
- child_weight: bfloat16 [32768], P(('grp', 'blk')), may hold values from 0.099609375 to 0.5
- child_slot: int32 [32768], P(('grp', 'blk')), may hold values from 0 to 639, as said below
- send_list: int32 [32, 640], P(('grp', 'blk')), may hold values from -1 to 255, as said below
- theta: float32 [32, 256], P('grp', 'blk'), may hold values from 0.05 to 0.24
Outputs:
- corrected: float32 [32, 256, 384], P('grp', 'blk')
Inputs may be any that keep to these rules, and one draw needn't show every extreme that they name: `send_list`: row v lists, for each of its 5 nearby owners k = 0, 1, ... in turn, 128 slots: used slots first, each holding a distinct local parent number e of that owner, then -1 for unused slots; every device uses at least one slot for each nearby owner, and in every device's row one nearby owner has all 128 slots used. `child_slot`: A child's slot is k * 128 + position and is a used slot of its device's row of send_list.
All inputs are finite; a program needn't handle non-finite values.
Results may differ from a plain program's by a relative error of at most 0.0007.
Values sent between devices are 32-bit elements; how exact they have to be, the bound alone decides.
A program may use at most 64 MiB of HBM per device.

v0:
```python
import jax
import jax.numpy as jnp
from jax import lax
from jax.sharding import PartitionSpec as P

PR = 8
PCOL = 32
HALF = 2
CAP = 128


def from_behind(x, axis, by):
    size = lax.axis_size(axis)
    return lax.ppermute(x, axis, [(i, (i + by) % size) for i in range(size)])


def with_halo(cells, sides, width):
    for axis, dim in sides:
        count = lax.axis_size(axis)
        ends = count - 1
        head = lax.slice_in_dim(cells, 0, width, axis=dim)
        tail = lax.slice_in_dim(cells, cells.shape[dim] - width, cells.shape[dim], axis=dim)
        cells = jnp.concatenate(
            [
                lax.ppermute(tail, axis, [(i, (i + 1) % count) for i in range(ends)]),
                cells,
                lax.ppermute(head, axis, [((i + 1) % count, i) for i in range(ends)]),
            ],
            axis=dim,
        )
    return cells


def body(child_field, child_weight, child_slot, send_list, theta):
    cells = PR * PCOL
    channels = child_field.shape[1]
    reach = 2 * HALF + 1
    slot_row = send_list.reshape(-1)
    restricted = jnp.zeros((cells, channels), jnp.float32)
    slot_ids = jnp.arange(reach * CAP, dtype=jnp.int32)
    matrix = jnp.where(
        slot_ids[:, None] == child_slot[None, :], child_weight[None, :], jnp.zeros((), jnp.bfloat16)
    )
    partial_value = jnp.dot(matrix, child_field, preferred_element_type=jnp.float32)
    entries = slot_row.reshape(reach, CAP)
    cell_ids = jnp.arange(cells, dtype=jnp.int32)
    for offset in range(reach):
        piece = partial_value[offset * CAP : (offset + 1) * CAP]
        numbers = entries[offset]
        if offset != HALF:
            numbers = from_behind(numbers, "blk", offset - HALF)
            piece = from_behind(piece, "blk", offset - HALF)
        selector = (cell_ids[:, None] == numbers[None, :]).astype(jnp.float32)
        restricted = restricted + jnp.dot(
            selector, piece, precision=lax.Precision.HIGHEST, preferred_element_type=jnp.float32
        )
    restricted = restricted.reshape(PR, PCOL, channels)
    padded = with_halo(restricted, (("grp", 0), ("blk", 1)), 1)
    beside = padded[2:, 1:-1] + padded[:-2, 1:-1] + padded[1:-1, 2:] + padded[1:-1, :-2]
    return restricted + theta[:, :, None] * (beside - 4.0 * restricted)


def solution(mesh):
    return jax.shard_map(
        body,
        mesh=mesh,
        in_specs=(
            P(("grp", "blk"), None),
            P(("grp", "blk")),
            P(("grp", "blk")),
            P(("grp", "blk"), None),
            P("grp", "blk"),
        ),
        out_specs=P("grp", "blk", None),
        check_vma=False,
    )
```

profile of v0, /device:TPU:9, one launch (start us, length us, event | category | flops | bytes accessed | tf_op | source)
XLA Modules:
  0.0 48.8 jit_solution(15430179811652947788)
XLA Ops:
  0.0 0.0 copy-start
  0.0 0.8 %slice_bitcast_fusion.3 = (s32[128]{0:T(128)S(1)}, s32[128]{0:T(128)S(1)}, s32[128]{0:T(128)S(1)}, s32[128]{0:T(128)S(1)}, s32[128]{0:T(128)S(1)}) fusion(s32[1,640]{1,0:T(1,128)} %param.8), kind=kLoop, calls=%fused_computation.44 | loop fusion | bytes 5120 | tf_op jit(solution)/shard_map/squeeze | solution.py:49
  0.8 1.2 %collective-permute-start.4 = (s32[128]{0:T(128)S(1)}, s32[128]{0:T(128)S(1)}, u32[]{:S(2)}, u32[]{:S(2)}) collective-permute-start(s32[128]{0:T(128)S(1)} %get-tuple-element.13), channel_id=1, source_target_pairs={{0,1},{1,2},{2,3},{3,4},{4,5},{5,6},{6,7},{7,0},{8,9},{9,10},{10,1... | collective-permute-start | bytes 1544 | tf_op jit(solution)/shard_map/ppermute | solution.py:14
  2.0 1.2 %collective-permute-start.2 = (s32[128]{0:T(128)S(1)}, s32[128]{0:T(128)S(1)}, u32[]{:S(2)}, u32[]{:S(2)}) collective-permute-start(s32[128]{0:T(128)S(1)} %get-tuple-element.15), channel_id=1, source_target_pairs={{0,7},{1,0},{2,1},{3,2},{4,3},{5,4},{6,5},{7,6},{8,15},{9,8},{10,9... | collective-permute-start | bytes 1544 | tf_op jit(solution)/shard_map/ppermute | solution.py:14
  3.2 2.1 %collective-permute-start = (s32[128]{0:T(128)S(1)}, s32[128]{0:T(128)S(1)}, u32[]{:S(2)}, u32[]{:S(2)}) collective-permute-start(s32[128]{0:T(128)S(1)} %get-tuple-element.16), channel_id=1, source_target_pairs={{0,6},{1,7},{2,0},{3,1},{4,2},{5,3},{6,4},{7,5},{8,14},{9,15},{10,... | collective-permute-start | bytes 1544 | tf_op jit(solution)/shard_map/ppermute | solution.py:14
  5.3 0.0 collective-permute-start.6
  5.3 0.0 copy-done
  5.3 1.5 %fusion.1 = f32[640,384]{1,0:T(8,128)S(1)} fusion(bf16[1024,384]{1,0:T(8,128)(2,1)S(1)} %copy-done, s32[1024]{0:T(1024)} %param.7, bf16[1024]{0:T(1024)(128)(2,1)} %param.6), kind=kOutput, calls=%fused_computation.2 | convolution fusion | flops 504627200 | bytes 1775616 | tf_op jit(solution)/shard_map/dot_general | solution.py:44
  6.8 0.1 fusion.24
  6.9 1.5 %collective-permute-start.3 = (f32[128,384]{1,0:T(8,128)S(1)}, f32[128,384]{1,0:T(8,128)S(1)}, u32[]{:S(2)}, u32[]{:S(2)}) collective-permute-start(f32[128,384]{1,0:T(8,128)S(1)} %get-tuple-element.7), channel_id=1, source_target_pairs={{0,7},{1,0},{2,1},{3,2},{4,3},{5,4},{6,5},{7,6},{8,15},{9,8},{10,9... | collective-permute-start | bytes 589832 | tf_op jit(solution)/shard_map/ppermute | solution.py:14
  8.3 0.3 fusion.14
  8.7 0.0 collective-permute-done.2
  8.7 0.1 collective-permute-start.5
  8.8 3.4 %collective-permute-done.3 = f32[128,384]{1,0:T(8,128)S(1)} collective-permute-done((f32[128,384]{1,0:T(8,128)S(1)}, f32[128,384]{1,0:T(8,128)S(1)}, u32[]{:S(2)}, u32[]{:S(2)}) %collective-permute-start.3) | collective-permute-done | bytes 196640 | tf_op jit(solution)/shard_map/ppermute | solution.py:14
  12.1 2.1 %collective-permute-start.1 = (f32[128,384]{1,0:T(8,128)S(1)}, f32[128,384]{1,0:T(8,128)S(1)}, u32[]{:S(2)}, u32[]{:S(2)}) collective-permute-start(f32[128,384]{1,0:T(8,128)S(1)} %get-tuple-element.8), channel_id=1, source_target_pairs={{0,6},{1,7},{2,0},{3,1},{4,2},{5,3},{6,4},{7,5},{8,14},{9,15},{10,... | collective-permute-start | bytes 589832 | tf_op jit(solution)/shard_map/ppermute | solution.py:14
  14.2 0.3 fusion.16
  14.6 0.0 collective-permute-done
  14.6 3.0 %collective-permute-start.7 = (f32[128,384]{1,0:T(8,128)S(1)}, f32[128,384]{1,0:T(8,128)S(1)}, u32[]{:S(2)}, u32[]{:S(2)}) collective-permute-start(f32[128,384]{1,0:T(8,128)S(1)} %get-tuple-element.6), channel_id=1, source_target_pairs={{0,2},{1,3},{2,4},{3,5},{4,6},{5,7},{6,0},{7,1},{8,10},{9,11},{10,... | collective-permute-start | bytes 589832 | tf_op jit(solution)/shard_map/ppermute | solution.py:14
  17.5 2.7 %collective-permute-done.1 = f32[128,384]{1,0:T(8,128)S(1)} collective-permute-done((f32[128,384]{1,0:T(8,128)S(1)}, f32[128,384]{1,0:T(8,128)S(1)}, u32[]{:S(2)}, u32[]{:S(2)}) %collective-permute-start.1) | collective-permute-done | bytes 196640 | tf_op jit(solution)/shard_map/ppermute | solution.py:14
  20.2 0.3 fusion.4
  20.5 0.0 collective-permute-done.6
  20.5 8.0 %collective-permute-done.7 = f32[128,384]{1,0:T(8,128)S(1)} collective-permute-done((f32[128,384]{1,0:T(8,128)S(1)}, f32[128,384]{1,0:T(8,128)S(1)}, u32[]{:S(2)}, u32[]{:S(2)}) %collective-permute-start.7) | collective-permute-done | bytes 196640 | tf_op jit(solution)/shard_map/ppermute | solution.py:14
  28.5 0.3 fusion.17
  28.8 0.0 copy-start.1
  28.8 0.0 collective-permute-done.4
  28.8 0.0 collective-permute-done.5
  28.9 0.3 fusion.5
  29.2 6.0 %collective-permute-start.9 = (f32[1,32,384]{2,1,0:T(8,128)S(1)}, f32[1,32,384]{2,1,0:T(8,128)S(1)}, u32[]{:S(2)}, u32[]{:S(2)}) collective-permute-start(f32[1,32,384]{2,1,0:T(8,128)S(1)} %get-tuple-element.11), channel_id=1, source_target_pairs={{0,8},{8,16},{16,24},{1,9},{9,17},{17,25},{2,10},{10,18},{18,26},{... | collective-permute-start | bytes 147464 | tf_op jit(solution)/shard_map/ppermute | solution.py:25
  35.2 1.9 %collective-permute-start.8 = (f32[1,32,384]{2,1,0:T(8,128)S(1)}, f32[1,32,384]{2,1,0:T(8,128)S(1)}, u32[]{:S(2)}, u32[]{:S(2)}) collective-permute-start(f32[1,32,384]{2,1,0:T(8,128)S(1)} %get-tuple-element.12), channel_id=1, source_target_pairs={{8,0},{16,8},{24,16},{9,1},{17,9},{25,17},{10,2},{18,10},{26,18},{... | collective-permute-start | bytes 147464 | tf_op jit(solution)/shard_map/ppermute | solution.py:27
  37.1 0.0 collective-permute-done.9
  37.1 3.5 %collective-permute-done.8 = f32[1,32,384]{2,1,0:T(8,128)S(1)} collective-permute-done((f32[1,32,384]{2,1,0:T(8,128)S(1)}, f32[1,32,384]{2,1,0:T(8,128)S(1)}, u32[]{:S(2)}, u32[]{:S(2)}) %collective-permute-start.8) | collective-permute-done | bytes 49184 | tf_op jit(solution)/shard_map/ppermute | solution.py:27
  40.6 1.9 %collective-permute-start.10 = (f32[10,1,384]{2,1,0:T(1,128)S(1)}, f32[10,1,384]{2,1,0:T(1,128)S(1)}, u32[]{:S(2)}, u32[]{:S(2)}) collective-permute-start(f32[10,1,384]{2,1,0:T(1,128)S(1)} %get-tuple-element.9), channel_id=1, source_target_pairs={{1,0},{2,1},{3,2},{4,3},{5,4},{6,5},{7,6},{9,8},{10,9},{11,10},{12... | collective-permute-start | bytes 46088 | tf_op jit(solution)/shard_map/ppermute | solution.py:27
  42.6 3.4 %collective-permute-start.11 = (f32[10,1,384]{2,1,0:T(1,128)S(1)}, f32[10,1,384]{2,1,0:T(1,128)S(1)}, u32[]{:S(2)}, u32[]{:S(2)}) collective-permute-start(f32[10,1,384]{2,1,0:T(1,128)S(1)} %get-tuple-element.10), channel_id=1, source_target_pairs={{0,1},{1,2},{2,3},{3,4},{4,5},{5,6},{6,7},{8,9},{9,10},{10,11},{11... | collective-permute-start | bytes 46088 | tf_op jit(solution)/shard_map/ppermute | solution.py:25
  45.9 0.0 collective-permute-done.10
  45.9 2.0 %collective-permute-done.11 = f32[10,1,384]{2,1,0:T(1,128)S(1)} collective-permute-done((f32[10,1,384]{2,1,0:T(1,128)S(1)}, f32[10,1,384]{2,1,0:T(1,128)S(1)}, u32[]{:S(2)}, u32[]{:S(2)}) %collective-permute-start.11) | collective-permute-done | bytes 15392 | tf_op jit(solution)/shard_map/ppermute | solution.py:25
  47.9 0.0 copy-done.1
  47.9 0.9 %fusion.11 = f32[8,32,384]{2,1,0:T(8,128)} fusion(f32[8,32,384]{2,1,0:T(8,128)S(1)} %bitcast.21, f32[10,1,384]{2,1,0:T(1,128)S(1)} %collective-permute-done.11, f32[1,32,384]{2,1,0:T(8,128)S(1)} %collective-permute-done.8, f32[1,32,384]{2,1,0:T(8,128)S(1)} %collective-permute-done.9, f32[10,1,384]{2,1,0:T(1,128)S(1)} %collective-permute-done.10, ...), kind=kLoop, calls=%fused_computation.14 | loop fusion | flops 1474560 | bytes 916480 | tf_op jit(solution)/shard_map/add | solution.py:60
  (2 shorter events, 0.0 us)
Async XLA Ops:
  0.0 5.3 %copy-start = (bf16[1024,384]{1,0:T(8,128)(2,1)S(1)}, bf16[1024,384]{1,0:T(8,128)(2,1)}, u32[]{:S(2)}) copy-start(bf16[1024,384]{1,0:T(8,128)(2,1)} %param.5) | copy-start | bytes 2359300
  0.8 28.0 %collective-permute-start.4 = (s32[128]{0:T(128)S(1)}, s32[128]{0:T(128)S(1)}, u32[]{:S(2)}, u32[]{:S(2)}) collective-permute-start(s32[128]{0:T(128)S(1)} %get-tuple-element.13), channel_id=1, source_target_pairs={{0,1},{1,2},{2,3},{3,4},{4,5},{5,6},{6,7},{7,0},{8,9},{9,10},{10,1... | collective-permute-start | bytes 1544 | tf_op jit(solution)/shard_map/ppermute | solution.py:14
  2.0 6.7 %collective-permute-start.2 = (s32[128]{0:T(128)S(1)}, s32[128]{0:T(128)S(1)}, u32[]{:S(2)}, u32[]{:S(2)}) collective-permute-start(s32[128]{0:T(128)S(1)} %get-tuple-element.15), channel_id=1, source_target_pairs={{0,7},{1,0},{2,1},{3,2},{4,3},{5,4},{6,5},{7,6},{8,15},{9,8},{10,9... | collective-permute-start | bytes 1544 | tf_op jit(solution)/shard_map/ppermute | solution.py:14
  3.2 11.4 %collective-permute-start = (s32[128]{0:T(128)S(1)}, s32[128]{0:T(128)S(1)}, u32[]{:S(2)}, u32[]{:S(2)}) collective-permute-start(s32[128]{0:T(128)S(1)} %get-tuple-element.16), channel_id=1, source_target_pairs={{0,6},{1,7},{2,0},{3,1},{4,2},{5,3},{6,4},{7,5},{8,14},{9,15},{10,... | collective-permute-start | bytes 1544 | tf_op jit(solution)/shard_map/ppermute | solution.py:14
  5.3 15.3 %collective-permute-start.6 = (s32[128]{0:T(128)S(1)}, s32[128]{0:T(128)S(1)}, u32[]{:S(2)}, u32[]{:S(2)}) collective-permute-start(s32[128]{0:T(128)S(1)} %get-tuple-element.17), channel_id=1, source_target_pairs={{0,2},{1,3},{2,4},{3,5},{4,6},{5,7},{6,0},{7,1},{8,10},{9,11},{10,... | collective-permute-start | bytes 1544 | tf_op jit(solution)/shard_map/ppermute | solution.py:14
  6.9 5.3 %collective-permute-start.3 = (f32[128,384]{1,0:T(8,128)S(1)}, f32[128,384]{1,0:T(8,128)S(1)}, u32[]{:S(2)}, u32[]{:S(2)}) collective-permute-start(f32[128,384]{1,0:T(8,128)S(1)} %get-tuple-element.7), channel_id=1, source_target_pairs={{0,7},{1,0},{2,1},{3,2},{4,3},{5,4},{6,5},{7,6},{8,15},{9,8},{10,9... | collective-permute-start | bytes 589832 | tf_op jit(solution)/shard_map/ppermute | solution.py:14
  8.7 20.2 %collective-permute-start.5 = (f32[128,384]{1,0:T(8,128)S(1)}, f32[128,384]{1,0:T(8,128)S(1)}, u32[]{:S(2)}, u32[]{:S(2)}) collective-permute-start(f32[128,384]{1,0:T(8,128)S(1)} %get-tuple-element.5), channel_id=1, source_target_pairs={{0,1},{1,2},{2,3},{3,4},{4,5},{5,6},{6,7},{7,0},{8,9},{9,10},{10,1... | collective-permute-start | bytes 589832 | tf_op jit(solution)/shard_map/ppermute | solution.py:14
  12.1 8.0 %collective-permute-start.1 = (f32[128,384]{1,0:T(8,128)S(1)}, f32[128,384]{1,0:T(8,128)S(1)}, u32[]{:S(2)}, u32[]{:S(2)}) collective-permute-start(f32[128,384]{1,0:T(8,128)S(1)} %get-tuple-element.8), channel_id=1, source_target_pairs={{0,6},{1,7},{2,0},{3,1},{4,2},{5,3},{6,4},{7,5},{8,14},{9,15},{10,... | collective-permute-start | bytes 589832 | tf_op jit(solution)/shard_map/ppermute | solution.py:14
  14.6 13.9 %collective-permute-start.7 = (f32[128,384]{1,0:T(8,128)S(1)}, f32[128,384]{1,0:T(8,128)S(1)}, u32[]{:S(2)}, u32[]{:S(2)}) collective-permute-start(f32[128,384]{1,0:T(8,128)S(1)} %get-tuple-element.6), channel_id=1, source_target_pairs={{0,2},{1,3},{2,4},{3,5},{4,6},{5,7},{6,0},{7,1},{8,10},{9,11},{10,... | collective-permute-start | bytes 589832 | tf_op jit(solution)/shard_map/ppermute | solution.py:14
  28.8 19.1 %copy-start.1 = (f32[8,32]{1,0:T(8,128)S(1)}, f32[8,32]{1,0:T(8,128)}, u32[]{:S(2)}) copy-start(f32[8,32]{1,0:T(8,128)} %param.9) | copy-start | bytes 3076
  29.2 7.9 %collective-permute-start.9 = (f32[1,32,384]{2,1,0:T(8,128)S(1)}, f32[1,32,384]{2,1,0:T(8,128)S(1)}, u32[]{:S(2)}, u32[]{:S(2)}) collective-permute-start(f32[1,32,384]{2,1,0:T(8,128)S(1)} %get-tuple-element.11), channel_id=1, source_target_pairs={{0,8},{8,16},{16,24},{1,9},{9,17},{17,25},{2,10},{10,18},{18,26},{... | collective-permute-start | bytes 147464 | tf_op jit(solution)/shard_map/ppermute | solution.py:25
  35.2 5.4 %collective-permute-start.8 = (f32[1,32,384]{2,1,0:T(8,128)S(1)}, f32[1,32,384]{2,1,0:T(8,128)S(1)}, u32[]{:S(2)}, u32[]{:S(2)}) collective-permute-start(f32[1,32,384]{2,1,0:T(8,128)S(1)} %get-tuple-element.12), channel_id=1, source_target_pairs={{8,0},{16,8},{24,16},{9,1},{17,9},{25,17},{10,2},{18,10},{26,18},{... | collective-permute-start | bytes 147464 | tf_op jit(solution)/shard_map/ppermute | solution.py:27
  40.6 5.3 %collective-permute-start.10 = (f32[10,1,384]{2,1,0:T(1,128)S(1)}, f32[10,1,384]{2,1,0:T(1,128)S(1)}, u32[]{:S(2)}, u32[]{:S(2)}) collective-permute-start(f32[10,1,384]{2,1,0:T(1,128)S(1)} %get-tuple-element.9), channel_id=1, source_target_pairs={{1,0},{2,1},{3,2},{4,3},{5,4},{6,5},{7,6},{9,8},{10,9},{11,10},{12... | collective-permute-start | bytes 46088 | tf_op jit(solution)/shard_map/ppermute | solution.py:27
  42.6 5.4 %collective-permute-start.11 = (f32[10,1,384]{2,1,0:T(1,128)S(1)}, f32[10,1,384]{2,1,0:T(1,128)S(1)}, u32[]{:S(2)}, u32[]{:S(2)}) collective-permute-start(f32[10,1,384]{2,1,0:T(1,128)S(1)} %get-tuple-element.10), channel_id=1, source_target_pairs={{0,1},{1,2},{2,3},{3,4},{4,5},{5,6},{6,7},{8,9},{9,10},{10,11},{11... | collective-permute-start | bytes 46088 | tf_op jit(solution)/shard_map/ppermute | solution.py:25
where the time goes:
time: 49.1 us; the launch traced here: 48.8 us
  starting transfers between devices  24.2 us (49%)
  waiting for transfers between devices  19.4 us (40%)
  matrix products  3.19 us (6%)
  other arithmetic  0.94 us (2%)
  local copies, waits for them, and re-layouts  0.87 us (2%)
    ppermute x8, waiting for transfers between devices, from_behind(): return lax.ppermute(x, axis, [(i, (i + by) % size) for i in range(size)])  14 us
    ppermute x8, starting transfers between devices, from_behind(): return lax.ppermute(x, axis, [(i, (i + by) % size) for i in range(size)])  11.1 us
    ppermute x2, starting transfers between devices, with_halo(): lax.ppermute(tail, axis, [(i, (i + 1) % count) for i in range(ends)])  9.32 us
    ppermute x2, starting transfers between devices, with_halo(): lax.ppermute(head, axis, [((i + 1) % count, i) for i in range(ends)])  3.84 us
    ppermute x2, waiting for transfers between devices, with_halo(): lax.ppermute(head, axis, [((i + 1) % count, i) for i in range(ends)])  3.47 us
    ppermute x2, waiting for transfers between devices, with_halo(): lax.ppermute(tail, axis, [(i, (i + 1) % count) for i in range(ends)])  1.99 us
    dot_general x5, matrix products, body(): jnp.dot(selector, piece, precision=lax.Precision.HIGHEST, preferred_eleme...  1.66 us
    dot_general x1, matrix products, body(): jnp.dot(matrix, child_field, preferred_element_type=jnp.float32)  1.54 us
  transfers between devices with their start and end apart: 12, of which 5 were waited for; matrix products, arithmetic and copies ran while one was open for 6% of the time, Pallas kernels for 0%

commit v1 on v0

v1 whole, which is shorter than its diff:
```python
import functools

import jax
import jax.numpy as jnp
from jax import lax
from jax.experimental import pallas as pl
from jax.experimental.pallas import tpu as pltpu
from jax.sharding import PartitionSpec as P

HALF = 2
LANES = 128
MESH = pl.DeviceIdType.MESH


def kernel(
    n_grp,
    n_blk,
    prows,
    pcols,
    cap,
    chunk,
    field_hbm,
    weight_hbm,
    slot_hbm,
    list_hbm,
    theta_hbm,
    out_ref,
    field,
    weight,
    slot,
    lists,
    theta,
    pieces,
    arrived,
    numbers,
    selector,
    restricted,
    theta_wide,
    edge_out,
    row_halo,
    col_halo,
    in_sem,
    num_send,
    num_recv,
    piece_send,
    piece_recv,
    halo_send,
    halo_recv,
):
    g = lax.axis_index("grp")
    b = lax.axis_index("blk")
    cells = prows * pcols
    chunks = restricted.shape[0]
    offsets = [o for o in (-1, 1, -2, 2)]

    def peer(offset):
        return (g, lax.rem(b + offset + n_blk, n_blk))

    barrier = pltpu.get_barrier_semaphore()
    for o in offsets:
        pl.semaphore_signal(barrier, inc=1, device_id=peer(o), device_id_type=MESH)

    @pl.when(g > 0)
    def _():
        pl.semaphore_signal(barrier, inc=1, device_id=(g - 1, b), device_id_type=MESH)

    @pl.when(g < n_grp - 1)
    def _():
        pl.semaphore_signal(barrier, inc=1, device_id=(g + 1, b), device_id_type=MESH)

    loads = [
        pltpu.make_async_copy(src, dst, in_sem.at[i])
        for i, (src, dst) in enumerate(
            [
                (slot_hbm, slot),
                (weight_hbm, weight),
                (field_hbm, field),
                (list_hbm, lists),
                (theta_hbm, theta),
            ]
        )
    ]
    for load in loads:
        load.start()
    @pl.when(g == 0)
    def _():
        row_halo[0] = jnp.zeros_like(row_halo[0])

    @pl.when(g == n_grp - 1)
    def _():
        row_halo[1] = jnp.zeros_like(row_halo[1])

    @pl.when(b == 0)
    def _():
        col_halo[0] = jnp.zeros_like(col_halo[0])

    @pl.when(b == n_blk - 1)
    def _():
        col_halo[1] = jnp.zeros_like(col_halo[1])

    loads[0].wait()
    loads[1].wait()
    slots = slot[...]
    weights = weight[...].astype(jnp.float32)
    groups = slots.shape[0]

    def weighted(k):
        ids = lax.broadcasted_iota(jnp.int32, (cap, LANES), 0) + k * cap
        return jnp.concatenate(
            [
                jnp.where(ids == slots[j : j + 1, :], weights[j : j + 1, :], 0.0).astype(jnp.bfloat16)
                for j in range(groups)
            ],
            axis=1,
        )

    def number_copy(i):
        return pltpu.make_async_remote_copy(
            src_ref=lists.at[:, pl.ds((HALF + offsets[i]) * cap, cap)],
            dst_ref=numbers.at[i],
            send_sem=num_send.at[i],
            recv_sem=num_recv.at[i],
            device_id=peer(offsets[i]),
            device_id_type=MESH,
        )

    def piece_copy(i, c):
        return pltpu.make_async_remote_copy(
            src_ref=pieces.at[i, c],
            dst_ref=arrived.at[i, c],
            send_sem=piece_send.at[i, c],
            recv_sem=piece_recv.at[i, c],
            device_id=peer(offsets[i]),
            device_id_type=MESH,
        )

    def make_piece(i, k):
        piece = jnp.dot(weighted(k), field[...], preferred_element_type=jnp.float32)
        for c in range(chunks):
            pieces[i, c] = piece[:, c * chunk : (c + 1) * chunk]

    loads[2].wait()
    loads[3].wait()
    make_piece(0, HALF + offsets[0])
    greeted = 4 + (g > 0).astype(jnp.int32) + (g < n_grp - 1).astype(jnp.int32)
    pl.semaphore_wait(barrier, greeted)
    for c in range(chunks):
        piece_copy(0, c).start()
    number_copy(0).start()
    for i in range(1, 4):
        make_piece(i, HALF + offsets[i])
        for c in range(chunks):
            piece_copy(i, c).start()
        number_copy(i).start()
    make_piece(4, HALF)

    loads[4].wait()
    diagonal = lax.broadcasted_iota(jnp.int32, (pcols, pcols), 0) == lax.broadcasted_iota(
        jnp.int32, (pcols, pcols), 1
    )
    for r in range(prows):
        column = jnp.sum(jnp.where(diagonal, theta[r : r + 1, :], 0.0), axis=1, keepdims=True)
        theta_wide[r * pcols : (r + 1) * pcols, :] = jnp.broadcast_to(column, (pcols, chunk))

    def select(i, entries):
        hit = lax.broadcasted_iota(jnp.int32, (cells, cap), 0) == entries
        hit = jnp.where(hit, 1.0, 0.0).astype(jnp.bfloat16)
        selector[i] = jnp.concatenate([hit, hit], axis=1)

    def spread(i, piece):
        high = piece.astype(jnp.bfloat16)
        low = (piece - high.astype(jnp.float32)).astype(jnp.bfloat16)
        return jnp.dot(
            selector[i], jnp.concatenate([high, low], axis=0), preferred_element_type=jnp.float32
        )

    select(4, lists[:, HALF * cap : (HALF + 1) * cap])
    for c in range(chunks):
        restricted[c] = spread(4, pieces[4, c])
    for i in range(4):
        number_copy(i).wait_recv()
        select(i, numbers[i])

    def row_copy(side, c):
        start = 0 if side else cells - pcols
        return pltpu.make_async_remote_copy(
            src_ref=restricted.at[c, pl.ds(start, pcols)],
            dst_ref=row_halo.at[side, c],
            send_sem=halo_send.at[side, c],
            recv_sem=halo_recv.at[side, c],
            device_id=(g - 1 if side else g + 1, b),
            device_id_type=MESH,
        )

    def col_copy(side, c):
        return pltpu.make_async_remote_copy(
            src_ref=edge_out.at[side, c],
            dst_ref=col_halo.at[side, c],
            send_sem=halo_send.at[2 + side, c],
            recv_sem=halo_recv.at[2 + side, c],
            device_id=(g, b - 1 if side else b + 1),
            device_id_type=MESH,
        )

    sends = [
        (g < n_grp - 1, row_copy, 0),
        (g > 0, row_copy, 1),
        (b < n_blk - 1, col_copy, 0),
        (b > 0, col_copy, 1),
    ]
    gets = [
        (g > 0, row_copy, 0),
        (g < n_grp - 1, row_copy, 1),
        (b > 0, col_copy, 0),
        (b < n_blk - 1, col_copy, 1),
    ]

    def finish(c):
        for here, copy, side in gets:

            @pl.when(here)
            def _():
                copy(side, c).wait_recv()

        own = restricted[c]
        col = lax.rem(lax.broadcasted_iota(jnp.int32, (cells, chunk), 0), pcols)

        def widened(side):
            return jnp.broadcast_to(
                col_halo[side, c][:, None, :], (prows, pcols, chunk)
            ).reshape(cells, chunk)

        up = jnp.concatenate([row_halo[0, c], own[: cells - pcols]], axis=0)
        down = jnp.concatenate([own[pcols:], row_halo[1, c]], axis=0)
        left = jnp.where(col == 0, widened(0), pltpu.roll(own, 1, 0))
        right = jnp.where(col == pcols - 1, widened(1), pltpu.roll(own, cells - 1, 0))
        beside = down + up + right + left
        out_ref[:, c * chunk : (c + 1) * chunk] = own + theta_wide[...] * (beside - 4.0 * own)

    for c in range(chunks):
        for i in range(4):
            piece_copy(i, c).wait_recv()
            restricted[c] += spread(i, arrived[i, c])
        edge_out[0, c] = restricted[c, pl.ds(pcols - 1, prows, stride=pcols), :]
        edge_out[1, c] = restricted[c, pl.ds(0, prows, stride=pcols), :]
        for here, copy, side in reversed(sends):

            @pl.when(here)
            def _():
                copy(side, c).start()

        if c > 0:
            finish(c - 1)
    finish(chunks - 1)

    for i in range(4):
        number_copy(i).wait_send()
        for c in range(chunks):
            piece_copy(i, c).wait_send()
    for c in range(chunks):
        for here, copy, side in sends:

            @pl.when(here)
            def _():
                copy(side, c).wait_send()


def body(n_grp, n_blk, child_field, child_weight, child_slot, send_list, theta):
    children, channels = child_field.shape
    prows, pcols = theta.shape
    cells = prows * pcols
    cap = send_list.shape[1] // (2 * HALF + 1)
    chunk = LANES
    chunks = channels // chunk
    groups = children // LANES
    f32, bf16, i32 = jnp.float32, jnp.bfloat16, jnp.int32
    dma = pltpu.SemaphoreType.DMA
    out = pl.pallas_call(
        functools.partial(kernel, n_grp, n_blk, prows, pcols, cap, chunk),
        out_shape=jax.ShapeDtypeStruct((cells, channels), f32),
        in_specs=[pl.BlockSpec(memory_space=pl.ANY)] * 5,
        out_specs=pl.BlockSpec(memory_space=pltpu.VMEM),
        scratch_shapes=[
            pltpu.VMEM((children, channels), bf16),
            pltpu.VMEM((groups, LANES), bf16),
            pltpu.VMEM((groups, LANES), i32),
            pltpu.VMEM(send_list.shape, i32),
            pltpu.VMEM((prows, pcols), f32),
            pltpu.VMEM((5, chunks, cap, chunk), f32),
            pltpu.VMEM((4, chunks, cap, chunk), f32),
            pltpu.VMEM((4, 1, cap), i32),
            pltpu.VMEM((5, cells, 2 * cap), bf16),
            pltpu.VMEM((chunks, cells, chunk), f32),
            pltpu.VMEM((cells, chunk), f32),
            pltpu.VMEM((2, chunks, prows, chunk), f32),
            pltpu.VMEM((2, chunks, pcols, chunk), f32),
            pltpu.VMEM((2, chunks, prows, chunk), f32),
            dma((5,)),
            dma((4,)),
            dma((4,)),
            dma((4, chunks)),
            dma((4, chunks)),
            dma((4, chunks)),
            dma((4, chunks)),
        ],
        compiler_params=pltpu.CompilerParams(collective_id=0, has_side_effects=True),
        name="nest_feedback",
    )(
        child_field,
        child_weight.reshape(groups, LANES),
        child_slot.reshape(groups, LANES),
        send_list,
        theta,
    )
    return out.reshape(prows, pcols, channels)


def solution(mesh):
    return jax.shard_map(
        functools.partial(body, mesh.shape["grp"], mesh.shape["blk"]),
        mesh=mesh,
        in_specs=(
            P(("grp", "blk"), None),
            P(("grp", "blk")),
            P(("grp", "blk")),
            P(("grp", "blk"), None),
            P("grp", "blk"),
        ),
        out_specs=P("grp", "blk", None),
        check_vma=False,
    )
```

time: 49.1 us -> 31.1 us (0.63)
  the two profiles are of different devices: /device:TPU:9 before, /device:TPU:0 now
where the time goes in v1:
time: 31.1 us; the launch traced here: 30.8 us
  Pallas kernels  29 us (93%)
  local copies, waits for them, and re-layouts  1.77 us (6%)
    pallas_call x1, Pallas kernels, body(): pl.pallas_call(functools.partial(kernel, n_grp, n_blk, prows, pcols, cap,...  29 us
    unnamed x1, local copies, waits for them, and re-layouts  1.77 us

profile of v1, /device:TPU:0, one launch (start us, length us, event | category | flops | bytes accessed | tf_op | source)
XLA Modules:
  0.0 30.8 jit_solution(3706753104026433919)
XLA Ops:
  0.0 29.0 %nest_feedback.1 = f32[256,384]{1,0:T(8,128)} custom-call(bf16[1024,384]{1,0:T(8,128)(2,1)} %field_hbm.1, bf16[8,128]{1,0:T(8,128)(2,1)} %bitcast.5, s32[8,128]{1,0:T(8,128)} %bitcast.4, s32[1,640]{1,0:T(1,128)} %list_hbm.1, f32[8,32]{1,0:T(8,128)} %theta_hbm.1), custom_call_target="tpu_custom_call" | custom-call | tf_op jit(solution)/shard_map/nest_feedback/pallas_call | solution.py:278
  29.0 1.8 %copy.7 = f32[8,32,384]{2,1,0:T(8,128)} copy(f32[8,32,384]{2,1,0:T(8,128)} %bitcast.3) | data formatting | bytes 786432

commit v2 on v1

--- a/solution.py
+++ b/solution.py
@@ -144,14 +144,15 @@
     make_piece(0, HALF + offsets[0])
     greeted = 4 + (g > 0).astype(jnp.int32) + (g < n_grp - 1).astype(jnp.int32)
     pl.semaphore_wait(barrier, greeted)
-    for c in range(chunks):
-        piece_copy(0, c).start()
-    number_copy(0).start()
+    for i in range(4):
+        number_copy(i).start()
+    piece_copy(0, 0).start()
     for i in range(1, 4):
         make_piece(i, HALF + offsets[i])
-        for c in range(chunks):
+        piece_copy(i, 0).start()
+    for c in range(1, chunks):
+        for i in range(4):
             piece_copy(i, c).start()
-        number_copy(i).start()
     make_piece(4, HALF)
 
     loads[4].wait()
@@ -277,8 +278,8 @@
     dma = pltpu.SemaphoreType.DMA
     out = pl.pallas_call(
         functools.partial(kernel, n_grp, n_blk, prows, pcols, cap, chunk),
-        out_shape=jax.ShapeDtypeStruct((cells, channels), f32),
-        in_specs=[pl.BlockSpec(memory_space=pl.ANY)] * 5,
+        out_shape=pltpu.VMEM((cells, channels), f32),
+        in_specs=[pl.BlockSpec(memory_space=pltpu.HBM)] * 5,
         out_specs=pl.BlockSpec(memory_space=pltpu.VMEM),
         scratch_shapes=[
             pltpu.VMEM((children, channels), bf16),
@@ -303,14 +304,19 @@
             dma((4, chunks)),
             dma((4, chunks)),
         ],
-        compiler_params=pltpu.CompilerParams(collective_id=0, has_side_effects=True),
+        compiler_params=pltpu.CompilerParams(collective_id=0, has_side_effects=True, vmem_limit_bytes=32 * 1024 * 1024),
         name="nest_feedback",
     )(
-        child_field,
-        child_weight.reshape(groups, LANES),
-        child_slot.reshape(groups, LANES),
-        send_list,
-        theta,
+        *[
+            pltpu.with_memory_space_constraint(x, pltpu.HBM)
+            for x in (
+                child_field,
+                child_weight.reshape(groups, LANES),
+                child_slot.reshape(groups, LANES),
+                send_list,
+                theta,
+            )
+        ]
     )
     return out.reshape(prows, pcols, channels)
 

time: 31.1 us -> 25.4 us (0.82)
  Pallas kernels: 29 us -> 24.4 us
  local copies, waits for them, and re-layouts: 1.77 us -> 0.75 us
    pallas_call x1, Pallas kernels: 29 us -> 24.4 us  [body(): pl.pallas_call(functools.partial(kernel, n_grp, n_blk, prows, pcols, cap,...]
    unnamed x1, local copies, waits for them, and re-layouts: 1.77 us -> 0.75 us
where the time goes in v2:
time: 25.4 us; the launch traced here: 25.2 us
  Pallas kernels  24.4 us (96%)
  local copies, waits for them, and re-layouts  0.75 us (3%)
    pallas_call x1, Pallas kernels, body(): pl.pallas_call(functools.partial(kernel, n_grp, n_blk, prows, pcols, cap,...  24.4 us
    unnamed x1, local copies, waits for them, and re-layouts  0.75 us

profile of v2, /device:TPU:0, one launch (start us, length us, event | category | flops | bytes accessed | tf_op | source)
XLA Modules:
  0.0 25.2 jit_solution(6099431161367614629)
XLA Ops:
  0.0 24.4 %nest_feedback.1 = f32[256,384]{1,0:T(8,128)S(1)} custom-call(bf16[1024,384]{1,0:T(8,128)(2,1)} %field_hbm.1, bf16[8,128]{1,0:T(8,128)(2,1)} %bitcast.5, s32[8,128]{1,0:T(8,128)} %bitcast.4, s32[1,640]{1,0:T(1,128)} %list_hbm.1, f32[8,32]{1,0:T(8,128)} %theta_hbm.1), custom_call_target="tpu_custom_call" | custom-call | tf_op jit(solution)/shard_map/nest_feedback/pallas_call | solution.py:279
  24.5 0.7 %copy.7 = f32[8,32,384]{2,1,0:T(8,128)} copy(f32[8,32,384]{2,1,0:T(8,128)S(1)} %bitcast.3) | data formatting | bytes 786432

commit v3 on v2

--- a/solution.py
+++ b/solution.py
@@ -33,6 +33,7 @@
     pieces,
     arrived,
     numbers,
+    weighted,
     selector,
     restricted,
     theta_wide,
@@ -74,14 +75,22 @@
             [
                 (slot_hbm, slot),
                 (weight_hbm, weight),
-                (field_hbm, field),
                 (list_hbm, lists),
                 (theta_hbm, theta),
             ]
         )
     ]
-    for load in loads:
+
+    def field_load(c):
+        return pltpu.make_async_copy(
+            field_hbm.at[:, pl.ds(c * chunk, chunk)], field.at[c], in_sem.at[len(loads) + c]
+        )
+
+    for load in loads[:3]:
         load.start()
+    for c in range(chunks):
+        field_load(c).start()
+    loads[3].start()
     @pl.when(g == 0)
     def _():
         row_halo[0] = jnp.zeros_like(row_halo[0])
@@ -104,15 +113,14 @@
     weights = weight[...].astype(jnp.float32)
     groups = slots.shape[0]
 
-    def weighted(k):
+    owners = weighted.shape[0] // cap
+    for k in range(owners):
         ids = lax.broadcasted_iota(jnp.int32, (cap, LANES), 0) + k * cap
-        return jnp.concatenate(
-            [
-                jnp.where(ids == slots[j : j + 1, :], weights[j : j + 1, :], 0.0).astype(jnp.bfloat16)
-                for j in range(groups)
-            ],
-            axis=1,
-        )
+        for j in range(groups):
+            hit = jnp.where(ids == slots[j : j + 1, :], weights[j : j + 1, :], 0.0)
+            weighted[k * cap : (k + 1) * cap, j * LANES : (j + 1) * LANES] = hit.astype(
+                jnp.bfloat16
+            )
 
     def number_copy(i):
         return pltpu.make_async_remote_copy(
@@ -124,38 +132,46 @@
             device_id_type=MESH,
         )
 
+    def reach_of(i):
+        if isinstance(i, int):
+            return offsets[i]
+        return jnp.where(i < 2, 2 * i - 1, 4 * i - 10)
+
     def piece_copy(i, c):
         return pltpu.make_async_remote_copy(
             src_ref=pieces.at[i, c],
             dst_ref=arrived.at[i, c],
             send_sem=piece_send.at[i, c],
             recv_sem=piece_recv.at[i, c],
-            device_id=peer(offsets[i]),
+            device_id=peer(reach_of(i)),
             device_id_type=MESH,
         )
 
-    def make_piece(i, k):
-        piece = jnp.dot(weighted(k), field[...], preferred_element_type=jnp.float32)
-        for c in range(chunks):
-            pieces[i, c] = piece[:, c * chunk : (c + 1) * chunk]
+    def make_pieces(c):
+        field_load(c).wait()
+        made = jnp.dot(weighted[...], field[c], preferred_element_type=jnp.float32)
+        for i, o in enumerate([*offsets, 0]):
+            pieces[i, c] = made[(HALF + o) * cap : (HALF + o + 1) * cap]
 
     loads[2].wait()
-    loads[3].wait()
-    make_piece(0, HALF + offsets[0])
+    make_pieces(0)
     greeted = 4 + (g > 0).astype(jnp.int32) + (g < n_grp - 1).astype(jnp.int32)
     pl.semaphore_wait(barrier, greeted)
     for i in range(4):
         number_copy(i).start()
-    piece_copy(0, 0).start()
-    for i in range(1, 4):
-        make_piece(i, HALF + offsets[i])
-        piece_copy(i, 0).start()
-    for c in range(1, chunks):
-        for i in range(4):
+    for c in range(chunks):
+        if c > 0:
+            make_pieces(c)
+        odd = lax.rem(b, 2)
+        far = 2 + (b >= n_blk - 2).astype(jnp.int32)
+        for i in (odd, 1 - odd, far):
             piece_copy(i, c).start()
-    make_piece(4, HALF)
-
-    loads[4].wait()
+        if c > 0:
+            piece_copy(5 - far, c - 1).start()
+        if c == chunks - 1:
+            piece_copy(5 - far, c).start()
+
+    loads[3].wait()
     diagonal = lax.broadcasted_iota(jnp.int32, (pcols, pcols), 0) == lax.broadcasted_iota(
         jnp.int32, (pcols, pcols), 1
     )
@@ -250,9 +266,8 @@
             def _():
                 copy(side, c).start()
 
-        if c > 0:
-            finish(c - 1)
-    finish(chunks - 1)
+    for c in range(chunks):
+        finish(c)
 
     for i in range(4):
         number_copy(i).wait_send()
@@ -282,7 +297,7 @@
         in_specs=[pl.BlockSpec(memory_space=pltpu.HBM)] * 5,
         out_specs=pl.BlockSpec(memory_space=pltpu.VMEM),
         scratch_shapes=[
-            pltpu.VMEM((children, channels), bf16),
+            pltpu.VMEM((chunks, children, chunk), bf16),
             pltpu.VMEM((groups, LANES), bf16),
             pltpu.VMEM((groups, LANES), i32),
             pltpu.VMEM(send_list.shape, i32),
@@ -290,13 +305,14 @@
             pltpu.VMEM((5, chunks, cap, chunk), f32),
             pltpu.VMEM((4, chunks, cap, chunk), f32),
             pltpu.VMEM((4, 1, cap), i32),
+            pltpu.VMEM((send_list.shape[1], children), bf16),
             pltpu.VMEM((5, cells, 2 * cap), bf16),
             pltpu.VMEM((chunks, cells, chunk), f32),
             pltpu.VMEM((cells, chunk), f32),
             pltpu.VMEM((2, chunks, prows, chunk), f32),
             pltpu.VMEM((2, chunks, pcols, chunk), f32),
             pltpu.VMEM((2, chunks, prows, chunk), f32),
-            dma((5,)),
+            dma((4 + chunks,)),
             dma((4,)),
             dma((4,)),
             dma((4, chunks)),

time: 25.4 us -> 23.5 us (0.925)
  Pallas kernels: 24.4 us -> 22.5 us
    pallas_call x1, Pallas kernels: 24.4 us -> 22.5 us  [body(): pl.pallas_call(functools.partial(kernel, n_grp, n_blk, prows, pcols, cap,...]
where the time goes in v3:
time: 23.5 us; the launch traced here: 23.3 us
  Pallas kernels  22.5 us (96%)
  local copies, waits for them, and re-layouts  0.75 us (3%)
    pallas_call x1, Pallas kernels, body(): pl.pallas_call(functools.partial(kernel, n_grp, n_blk, prows, pcols, cap,...  22.5 us
    unnamed x1, local copies, waits for them, and re-layouts  0.75 us

profile of v3, /device:TPU:0, one launch (start us, length us, event | category | flops | bytes accessed | tf_op | source)
XLA Modules:
  0.0 23.3 jit_solution(2903587216352358981)
XLA Ops:
  0.0 22.5 %nest_feedback.1 = f32[256,384]{1,0:T(8,128)S(1)} custom-call(bf16[1024,384]{1,0:T(8,128)(2,1)} %field_hbm.1, bf16[8,128]{1,0:T(8,128)(2,1)} %bitcast.5, s32[8,128]{1,0:T(8,128)} %bitcast.4, s32[1,640]{1,0:T(1,128)} %list_hbm.1, f32[8,32]{1,0:T(8,128)} %theta_hbm.1), custom_call_target="tpu_custom_call" | custom-call | tf_op jit(solution)/shard_map/nest_feedback/pallas_call | solution.py:294
  22.5 0.7 %copy.7 = f32[8,32,384]{2,1,0:T(8,128)} copy(f32[8,32,384]{2,1,0:T(8,128)S(1)} %bitcast.3) | data formatting | bytes 786432

commit v4 on v3

--- a/solution.py
+++ b/solution.py
@@ -163,7 +163,7 @@
         if c > 0:
             make_pieces(c)
         odd = lax.rem(b, 2)
-        far = 2 + (b >= n_blk - 2).astype(jnp.int32)
+        far = 2 + (b >= n_blk // 2).astype(jnp.int32)
         for i in (odd, 1 - odd, far):
             piece_copy(i, c).start()
         if c > 0:
@@ -255,7 +255,7 @@
         out_ref[:, c * chunk : (c + 1) * chunk] = own + theta_wide[...] * (beside - 4.0 * own)
 
     for c in range(chunks):
-        for i in range(4):
+        for i in (0, 1, 2, 3):
             piece_copy(i, c).wait_recv()
             restricted[c] += spread(i, arrived[i, c])
         edge_out[0, c] = restricted[c, pl.ds(pcols - 1, prows, stride=pcols), :]

time: 23.5 us -> 23.5 us (level)
  no operation moved by 1% of the time
where the time goes in v4:
time: 23.5 us; the launch traced here: 23.3 us
  Pallas kernels  22.5 us (96%)
  local copies, waits for them, and re-layouts  0.75 us (3%)
    pallas_call x1, Pallas kernels, body(): pl.pallas_call(functools.partial(kernel, n_grp, n_blk, prows, pcols, cap,...  22.5 us
    unnamed x1, local copies, waits for them, and re-layouts  0.75 us

profile of v4, /device:TPU:0, one launch (start us, length us, event | category | flops | bytes accessed | tf_op | source)
XLA Modules:
  0.0 23.3 jit_solution(12847438556963443834)
XLA Ops:
  0.0 22.5 %nest_feedback.1 = f32[256,384]{1,0:T(8,128)S(1)} custom-call(bf16[1024,384]{1,0:T(8,128)(2,1)} %field_hbm.1, bf16[8,128]{1,0:T(8,128)(2,1)} %bitcast.5, s32[8,128]{1,0:T(8,128)} %bitcast.4, s32[1,640]{1,0:T(1,128)} %list_hbm.1, f32[8,32]{1,0:T(8,128)} %theta_hbm.1), custom_call_target="tpu_custom_call" | custom-call | tf_op jit(solution)/shard_map/nest_feedback/pallas_call | solution.py:294
  22.5 0.7 %copy.7 = f32[8,32,384]{2,1,0:T(8,128)} copy(f32[8,32,384]{2,1,0:T(8,128)S(1)} %bitcast.3) | data formatting | bytes 786432
